TPU v7x, 32 devices: a whole 2x2x4 slice. The times are simulated.
32 devices in a mesh: chan: 4 (over z), tile: 8 (over y, x, core).
Axes of the slice: x: 2, y: 2, z: 4, core: 2. Of those that a mesh axis runs over, the one named last changes fastest.
Arguments:
- visibility: bfloat16 [1024, 2, 1024], P('tile', None, 'chan'), may hold values from -6 to 6
- flags: int32 [1024, 1024], P('tile', 'chan'), may hold values 0 or 1
- u_index: int32 [1024], replicated, may hold values from 0 to 511
- v_index: int32 [1024], replicated, may hold values from 0 to 255
- fg_filter: bfloat16 [1024, 1024], replicated, may hold values from -1 to 1
Outputs:
- cleaned: float32 [1024, 2, 1024], P('tile', None, 'chan')
All inputs are finite; a program needn't handle non-finite values. No bound on the sum of `flags` on one device may be relied on, other than what follows from the above.
Results may differ from a plain program's by a relative error of at most 0.0029.
Values may be sent and summed in bfloat16 or wider, within the bound.
No kernel may reach another device: no remote copies, remote signals or barrier semaphores. Data moves between devices by JAX's collectives and lax.ppermute only.
A program may use at most 256 MiB of HBM per device.

v0:
```python
import math
import jax
import jax.numpy as jnp
from jax import lax
from jax.sharding import PartitionSpec as P

F = 1024
L = 512
M = 256
TWO_PI = 2.0 * math.pi
FINE_STEP = 8


def tables(grid_index, positions, period):
    turn_count = grid_index[:, None] * positions[None, :] % period
    angles = turn_count.astype(jnp.float32) * (TWO_PI / period)
    return (jnp.cos(angles).astype(jnp.bfloat16), jnp.sin(angles).astype(jnp.bfloat16))


def line_tables(u_rows, line_ids, chan_start, chan_count, chan_total, line_total):
    period = chan_total * line_total
    coarse_ids = (
        chan_total + chan_start + FINE_STEP * jnp.arange(chan_count // FINE_STEP, dtype=jnp.int32)
    )
    fine_ids = jnp.arange(FINE_STEP, dtype=jnp.int32)
    base = u_rows[:, None] * line_ids[None, :]
    coarse_turns = base[:, :, None] * coarse_ids[None, None, :] % period
    fine_turns = base[:, :, None] * fine_ids[None, None, :] % period
    coarse_angle = coarse_turns.astype(jnp.float32) * (TWO_PI / period)
    fine_angle = fine_turns.astype(jnp.float32) * (TWO_PI / period)
    coarse_cos = jnp.cos(coarse_angle)[:, :, :, None]
    coarse_sin = jnp.sin(coarse_angle)[:, :, :, None]
    fine_cos = jnp.cos(fine_angle)[:, :, None, :]
    fine_sin = jnp.sin(fine_angle)[:, :, None, :]
    whole_cos = coarse_cos * fine_cos - coarse_sin * fine_sin
    whole_sin = coarse_sin * fine_cos + coarse_cos * fine_sin
    shape = (u_rows.shape[0], line_ids.shape[0], chan_count)
    return (
        whole_cos.reshape(shape).astype(jnp.bfloat16),
        whole_sin.reshape(shape).astype(jnp.bfloat16),
    )


def predict(image_lines, cos_line, sin_line, cos_col, sin_col):
    line_count, chan_count, pixel_cols = image_lines.shape
    row_count = cos_col.shape[0]
    phase_both = jnp.concatenate([cos_col, sin_col], 0)
    hidden_sum = lax.dot_general(
        image_lines.reshape(line_count * chan_count, pixel_cols),
        phase_both,
        (((1,), (1,)), ((), ())),
        preferred_element_type=jnp.float32,
    )
    hidden_sum = hidden_sum.reshape(line_count, chan_count, 2, row_count)
    half_cos = hidden_sum[:, :, 0, :]
    half_sin = hidden_sum[:, :, 1, :]
    row_cos = jnp.transpose(cos_line.astype(jnp.float32), (1, 2, 0))
    row_sin = jnp.transpose(sin_line.astype(jnp.float32), (1, 2, 0))
    real_pred = jnp.sum(row_cos * half_cos - row_sin * half_sin, axis=0)
    imag_pred = -jnp.sum(row_sin * half_cos + row_cos * half_sin, axis=0)
    return jnp.transpose(jnp.stack([real_pred, imag_pred], 0), (2, 0, 1))


def local(visibility, flags, u_index, v_index, fg_filter):
    row_count = visibility.shape[0]
    chan_count = visibility.shape[2]
    total_rows = u_index.shape[0]
    line_count = L // lax.axis_size("tile")
    line_ids = lax.axis_index("tile") * line_count + jnp.arange(line_count, dtype=jnp.int32)
    chan_start = lax.axis_index("chan") * chan_count
    cos_line, sin_line = line_tables(u_index, line_ids, chan_start, chan_count, F, L)
    cos_col, sin_col = tables(v_index, jnp.arange(M, dtype=jnp.int32), 2 * M)
    weight = flags.astype(jnp.bfloat16)
    weighted = visibility * weight[:, None, :]
    shard_piece = lax.all_gather(weighted, "tile", axis=0, tiled=True)
    piece_rows = shard_piece.shape[0]
    line_cos = cos_line.astype(jnp.float32)
    line_sin = sin_line.astype(jnp.float32)
    real_part = shard_piece[:, 0, :].astype(jnp.float32)[:, None, :]
    imag_part = shard_piece[:, 1, :].astype(jnp.float32)[:, None, :]
    x_real = (real_part * line_cos - imag_part * line_sin).astype(jnp.bfloat16)
    x_imag = (real_part * line_sin + imag_part * line_cos).astype(jnp.bfloat16)
    stacked = jnp.concatenate([x_real, x_imag], 0).reshape(2 * piece_rows, line_count * chan_count)
    phase_cols = jnp.concatenate([cos_col, -sin_col], 0)
    dirty_sum = lax.dot_general(
        stacked, phase_cols, (((0,), (0,)), ((), ())), preferred_element_type=jnp.float32
    )
    dirty_image = (
        (dirty_sum * (1.0 / math.sqrt(total_rows)))
        .astype(jnp.bfloat16)
        .reshape(line_count, chan_count, M)
    )
    filtered = jnp.einsum(
        "fg,qgm->qfm",
        fg_filter,
        lax.all_to_all(dirty_image, "chan", split_axis=0, concat_axis=1, tiled=True),
        preferred_element_type=jnp.float32,
    ).astype(jnp.bfloat16)
    foreground = lax.all_to_all(filtered, "chan", split_axis=1, concat_axis=0, tiled=True)
    own_start = lax.axis_index("tile") * row_count
    u_owned = lax.dynamic_slice_in_dim(u_index, own_start, row_count, 0)
    v_owned = lax.dynamic_slice_in_dim(v_index, own_start, row_count, 0)
    full_cos, full_sin = line_tables(
        u_owned, jnp.arange(L, dtype=jnp.int32), chan_start, chan_count, F, L
    )
    own_cos, own_sin = tables(v_owned, jnp.arange(M, dtype=jnp.int32), 2 * M)
    zero_rows = jnp.zeros((row_count, 2, chan_count), jnp.float32)
    shard_piece = lax.all_gather(foreground, "tile", axis=0, tiled=True)
    piece_lines = shard_piece.shape[0]
    block_count = piece_lines // line_count
    blocks = shard_piece.reshape(block_count, line_count, chan_count, M)
    offsets = jnp.arange(block_count, dtype=jnp.int32) * line_count

    def one_block(carried, scan_item):
        block_lines, offset = scan_item
        block_cos = lax.dynamic_slice_in_dim(full_cos, offset, line_count, 1)
        block_sin = lax.dynamic_slice_in_dim(full_sin, offset, line_count, 1)
        return (carried + predict(block_lines, block_cos, block_sin, own_cos, own_sin), None)

    summed, _ = lax.scan(one_block, zero_rows, (blocks, offsets))
    predicted = summed * (1.0 / math.sqrt(L * M))
    return weight.astype(jnp.float32)[:, None, :] * (visibility.astype(jnp.float32) - predicted)


def solution(mesh):
    return jax.shard_map(
        local,
        mesh=mesh,
        in_specs=(P("tile", None, "chan"), P("tile", "chan"), P(), P(), P()),
        out_specs=P("tile", None, "chan"),
        check_vma=False,
    )
```

profile of v0, /device:TPU:0, one launch (start us, length us, event | category | flops | bytes accessed | tf_op | source)
XLA Modules:
  0.0 1037.5 jit_solution(1772755833792879278)
XLA Ops:
  10.7 8.2 fusion.57
  18.9 34.4 %fusion.32 = (f32[1024,64,32]{0,2,1:T(8,128)}, f32[1024,64,32]{0,2,1:T(8,128)}) fusion(s32[32]{0:T(128)S(1)} %multiply_add_fusion, s32[1024,64]{0,1:T(8,128)S(1)} %broadcast_multiply_fusion), kind=kLoop, calls=%fused_computation.55 | loop fusion | flops 29360128 | bytes 17039488 | tf_op jit(solution)/shard_map/cos | solution.py:31
  53.4 27.3 %add_convert_fusion.1 = (bf16[1024,64,32,8]{0,3,2,1:T(8,128)(2,1)}, bf16[1024,64,32,8]{0,3,2,1:T(8,128)(2,1)}) fusion(f32[1024,64,8]{0,2,1:T(8,128)S(1)} %get-tuple-element.152, f32[1024,64,32]{0,2,1:T(8,128)} %get-tuple-element.148, f32[1024,64,8]{0,2,1:T(8,128)S(1)} %get-tuple-element.151, f32[1024,64,32]{0,2,1:T(8,128)} %get-tuple-element.147), kind=kLoop, calls=%fused_computation.30 | loop fusion | flops 134217728 | bytes 88080384 | tf_op jit(solution)/shard_map/convert_element_type | solution.py:40
  80.7 5.0 cosine_convert_fusion
  85.6 5.5 fusion.61
  97.9 46.6 %fusion.10 = (bf16[1024,16384]{0,1:T(8,128)(2,1)}, bf16[1024,16384]{0,1:T(8,128)(2,1)}) fusion(bf16[1024,64,32,8]{0,3,2,1:T(8,128)(2,1)} %get-tuple-element.144, bf16[1024,64,32,8]{0,3,2,1:T(8,128)(2,1)} %get-tuple-element.143, f32[1024,256]{0,1:T(8,128)} %copy.24, f32[1024,256]{0,1:T(8,128)S(1)} %copy.23), kind=kLoop, calls=%fused_computation.22 | loop fusion | flops 167772160 | bytes 136314880 | tf_op jit(solution)/shard_map/convert_element_type | solution.py:81
  144.5 28.8 %fusion.22 = bf16[16384,256]{1,0:T(8,128)(2,1)} fusion(bf16[1024,16384]{0,1:T(8,128)(2,1)} %get-tuple-element.140, bf16[1024,16384]{0,1:T(8,128)(2,1)} %get-tuple-element.139, bf16[1024,256]{1,0:T(8,128)(2,1)} %fusion.61, bf16[1024,256]{1,0:T(8,128)(2,1)} %cosine_convert_fusion), kind=kOutput, calls=%fused_computation.36 | convolution fusion | flops 17324572672 | bytes 76546048 | tf_op jit(solution)/shard_map/dot_general | solution.py:85
  173.3 192.2 %all_to_all.36 = bf16[64,256,256]{2,1,0:T(8,128)(2,1)} all-to-all(bf16[64,256,256]{2,1,0:T(8,128)(2,1)} %bitcast.133), channel_id=1, replica_groups=mesh['chan'=4,'tile'=8] {'chan'}, dimensions={0} | all-to-all | bytes 16777216 | tf_op jit(solution)/shard_map/all_to_all | solution.py:96
  365.5 13.7 %copy.25 = bf16[4,16,256,256]{2,0,3,1:T(4,128)(2,1)} copy(bf16[4,16,256,256]{3,2,1,0:T(8,128)(2,1)} %bitcast.129) | data formatting | bytes 16777216 | tf_op jit(solution)/shard_map/all_to_all | solution.py:96
  379.1 14.3 %all_to_all.29 = bf16[16,1024,256]{1,2,0:T(8,128)(2,1)} reshape(bf16[16,4,256,256]{2,1,3,0:T(4,128)(2,1)} %bitcast.130) | data formatting | bytes 16777216 | tf_op jit(solution)/shard_map/all_to_all | solution.py:96
  393.5 14.6 %convert_bitcast_fusion = bf16[16,1024,256]{1,2,0:T(8,128)(2,1)} fusion(bf16[16,1024,256]{1,2,0:T(8,128)(2,1)} %all_to_all.29, bf16[1024,1024]{1,0:T(8,128)(2,1)S(1)} %copy-done), kind=kOutput, calls=%fused_computation.53 | convolution fusion | flops 8594128896 | bytes 18874368 | tf_op jit(solution)/shard_map/fg,qgm->qfm/dot_general | solution.py:93
  408.1 12.6 %copy.26 = bf16[16,1024,256]{2,0,1:T(8,128)(2,1)} copy(bf16[16,1024,256]{1,2,0:T(8,128)(2,1)} %convert_bitcast_fusion) | data formatting | bytes 16777216 | tf_op jit(solution)/shard_map/convert_element_type | solution.py:98
  420.7 190.4 %all_to_all.37 = bf16[16,1024,256]{2,0,1:T(8,128)(2,1)} all-to-all(bf16[16,1024,256]{2,0,1:T(8,128)(2,1)} %copy.26), channel_id=1, replica_groups=mesh['chan'=4,'tile'=8] {'chan'}, dimensions={1} | all-to-all | bytes 16777216 | tf_op jit(solution)/shard_map/all_to_all | solution.py:99
  611.1 9.9 copy.28
  622.6 8.2 fusion.59
  630.8 34.7 %fusion.34 = (f32[128,512,32]{0,2,1:T(8,128)}, f32[128,512,32]{0,2,1:T(8,128)}) fusion(s32[32]{0:T(128)S(1)} %copy-done.6, s32[128,512]{0,1:T(8,128)S(1)} %iota_multiply_fusion), kind=kLoop, calls=%fused_computation.57 | loop fusion | flops 29360128 | bytes 17039488 | tf_op jit(solution)/shard_map/cos | solution.py:31
  665.5 27.5 %fusion.18 = (bf16[128,512,256]{0,2,1:T(8,128)(2,1)}, bf16[128,512,256]{0,2,1:T(8,128)(2,1)}) fusion(f32[128,512,8]{0,2,1:T(8,128)S(1)} %get-tuple-element.154, f32[128,512,32]{0,2,1:T(8,128)} %get-tuple-element.150, f32[128,512,8]{0,2,1:T(8,128)S(1)} %get-tuple-element.153, f32[128,512,32]{0,2,1:T(8,128)} %get-tuple-element.149), kind=kLoop, calls=%fused_computation.34 | loop fusion | flops 134217728 | bytes 88080384 | tf_op jit(solution)/shard_map/convert_element_type | solution.py:40
  693.0 229.7 %all-gather.5.cloned.1.call-done = bf16[512,256,256]{2,1,0:T(8,128)(2,1)} async-done(((bf16[64,256,256]{2,1,0:T(8,128)(2,1)}), bf16[512,256,256]{2,1,0:T(8,128)(2,1)}) %all-gather.5.cloned.1.call-update) | async-done | bytes 67108880 | tf_op jit(solution)/shard_map/all_gather | solution.py:108
  922.7 106.0 %while.13 = (s32[]{:T(128)}, f32[128,2,256]{0,2,1:T(8,128)S(1)}, s32[8]{0:T(128)S(1)}, bf16[128,512,256]{0,2,1:T(8,128)(2,1)}, bf16[8,64,256,256]{3,2,1,0:T(8,12...) while((s32[]{:T(128)}, f32[128,2,256]{0,2,1:T(8,128)S(1)}, ...), condition=%wide.region_3.4_spmd.clone, body=%wide.region_0.3_spmd.clone.sunk | while | flops 2168619008 | bytes 51774108 | solution.py:120
  925.4 4.8 fusion.84
  930.2 5.6 fusion.85
  943.4 5.6 fusion.85
  951.9 4.8 fusion.84
  956.7 5.6 fusion.85
  965.1 4.8 fusion.84
  970.0 5.6 fusion.85
  983.2 5.6 fusion.85
  991.7 4.8 fusion.84
  996.5 5.6 fusion.85
  1004.9 4.8 fusion.84
  1009.7 5.6 fusion.85
  1023.0 5.6 fusion.85
  (63 shorter events, 34.4 us)
Async XLA Ops:
  6.5 387.0 %copy-start = (bf16[1024,1024]{1,0:T(8,128)(2,1)S(1)}, bf16[1024,1024]{1,0:T(8,128)(2,1)}, u32[]{:S(2)}) copy-start(bf16[1024,1024]{1,0:T(8,128)(2,1)} %param.11) | copy-start | bytes 6291460
  6.5 84.6 %all-gather.3.cloned.1.call-start = ((), (), s32[]{:S(2)}) async-start(), calls=%async_computation.2 | async-start | bytes 1179648 | tf_op jit(solution)/shard_map/all_gather | solution.py:75
  9.9 912.8 %all-gather.5.cloned.1.call-start = ((), (), s32[]{:S(2)}) async-start(), calls=%async_computation.3 | async-start | bytes 75497472 | tf_op jit(solution)/shard_map/all_gather | solution.py:108
  9.9 43.4 %copy-start.5 = (s32[32]{0:T(128)}, s32[32]{0:T(128)S(1)}, u32[]{:S(2)}) copy-start(s32[32]{0:T(128)S(1)} %multiply_add_fusion) | copy-start | bytes 388
  53.4 27.3 %copy-start.4 = (s32[1024]{0:T(1024)S(1)}, s32[1024]{0:T(1024)}, u32[]{:S(2)}) copy-start(s32[1024]{0:T(1024)} %param.10) | copy-start | bytes 12292
  621.0 9.7 copy-start.6
  922.7 106.2 %copy-start.2 = (bf16[128,2,256]{2,1,0:T(2,128)(2,1)S(1)}, bf16[128,2,256]{2,1,0:T(2,128)(2,1)}, u32[]{:S(2)}) copy-start(bf16[128,2,256]{2,1,0:T(2,128)(2,1)} %param.7) | copy-start | bytes 393220
  922.7 106.2 %copy-start.3 = (f32[128,256]{1,0:T(8,128)S(1)}, f32[128,256]{1,0:T(8,128)}, u32[]{:S(2)}) copy-start(f32[128,256]{1,0:T(8,128)} %get-tuple-element.137) | copy-start | bytes 393220
  1028.7 1.7 copy-start.1
Sparse Core Ops, SparseCore 0:
  10.0 26.2 all-gather.2
  621.2 301.4 all-gather.4
where the time goes:
time: 1050 us; the launch traced here: 1040 us
  blocking collectives  383 us (36%)
  other arithmetic  251 us (24%)
  waiting for transfers between devices  230 us (22%)
  matrix products  81.8 us (8%)
  local copies, waits for them, and re-layouts  61.4 us (6%)
  loops' own time  16.6 us (2%)
  between operations  13.8 us (1%)
    all_gather x1, waiting for transfers between devices, local(): shard_piece = lax.all_gather(foreground, 'tile', axis=0, tiled=True)  230 us
    all_to_all x1, blocking collectives, local(): lax.all_to_all(dirty_image, 'chan', split_axis=0, concat_axis=1, tiled=True)  192 us
    all_to_all x1, blocking collectives, local(): lax.all_to_all(filtered, 'chan', split_axis=1, concat_axis=0, tiled=True)  190 us
    cos x2, other arithmetic, line_tables(): coarse_cos = jnp.cos(coarse_angle)[:, :, :, None]  69.1 us
    convert_element_type x2, other arithmetic, line_tables(): whole_sin.reshape(shape).astype(jnp.bfloat16)  54.8 us
    convert_element_type x1, other arithmetic, local(): x_real = (real_part * line_cos - imag_part * line_sin).astype(jnp.bfloat16)  46.6 us
    reduce_sum x8, other arithmetic, predict(): real_pred = jnp.sum(row_cos * half_cos - row_sin * half_sin, axis=0)  45 us
    dot_general x8, matrix products, predict(): lax.dot_general(image_lines.reshape(line_count * chan_count, pixel_cols),...  38.5 us
  transfers between devices with their start and end apart: 2, of which 1 were waited for; matrix products, arithmetic and copies ran while one was open for 15% of the time, Pallas kernels for 0%

commit v1 on v0

--- a/solution.py
+++ b/solution.py
@@ -9,6 +9,18 @@
 M = 256
 TWO_PI = 2.0 * math.pi
 FINE_STEP = 8
+
+
+def gather_around(array, axis, dim):
+    ways, here, step = (lax.axis_size(axis), lax.axis_index(axis), array.shape[dim])
+    shape = [n * ways if d == dim else n for d, n in enumerate(array.shape)]
+    full = lax.dynamic_update_slice_in_dim(
+        jnp.zeros(shape, array.dtype), array, here * step, axis=dim
+    )
+    for far in range(1, ways):
+        array = lax.ppermute(array, axis, [(d, (d + 1) % ways) for d in range(ways)])
+        full = lax.dynamic_update_slice_in_dim(full, array, (here - far) % ways * step, axis=dim)
+    return full
 
 
 def tables(grid_index, positions, period):
@@ -105,7 +117,7 @@
     )
     own_cos, own_sin = tables(v_owned, jnp.arange(M, dtype=jnp.int32), 2 * M)
     zero_rows = jnp.zeros((row_count, 2, chan_count), jnp.float32)
-    shard_piece = lax.all_gather(foreground, "tile", axis=0, tiled=True)
+    shard_piece = gather_around(foreground, "tile", 0)
     piece_lines = shard_piece.shape[0]
     block_count = piece_lines // line_count
     blocks = shard_piece.reshape(block_count, line_count, chan_count, M)

time: 1050 us -> 1440 us (1.37)
  waiting for transfers between devices: 230 us -> 527 us
  local copies, waits for them, and re-layouts: 61.4 us -> 156 us
    ppermute x0 -> x7, waiting for transfers between devices: none -> 527 us  [gather_around(): lax.ppermute(array, axis, [(d, (d + 1) % ways) for d in range(ways)])]
    all_gather x1 -> x0, waiting for transfers between devices: 230 us -> none  [local(): shard_piece = lax.all_gather(foreground, 'tile', axis=0, tiled=True)]
    dynamic_update_slice x0 -> x8, local copies, waits for them, and re-layouts: none -> 60.9 us  [the longest x7 53.3 us: gather_around(): lax.dynamic_update_slice_in_dim(full, array, (here - far) % ways * step,...]
    broadcast_in_dim x0 -> x1, local copies, waits for them, and re-layouts: none -> 20.9 us  [gather_around(): jnp.zeros(shape, array.dtype)]
  transfers between devices with their start and end apart: 2 -> 8, of which waited for: 1 -> 6; matrix products, arithmetic and copies ran while one was open for 15% -> 16% of each run, Pallas kernels for 0% -> 0%
where the time goes in v1:
time: 1440 us; the launch traced here: 1430 us
  waiting for transfers between devices  527 us (37%)
  blocking collectives  383 us (27%)
  other arithmetic  251 us (17%)
  local copies, waits for them, and re-layouts  156 us (11%)
  matrix products  81.9 us (6%)
    ppermute x7, waiting for transfers between devices, gather_around(): lax.ppermute(array, axis, [(d, (d + 1) % ways) for d in range(ways)])  527 us
    all_to_all x1, blocking collectives, local(): lax.all_to_all(dirty_image, 'chan', split_axis=0, concat_axis=1, tiled=True)  192 us
    all_to_all x1, blocking collectives, local(): lax.all_to_all(filtered, 'chan', split_axis=1, concat_axis=0, tiled=True)  190 us
    cos x2, other arithmetic, line_tables(): coarse_cos = jnp.cos(coarse_angle)[:, :, :, None]  69.1 us
    convert_element_type x2, other arithmetic, line_tables(): whole_sin.reshape(shape).astype(jnp.bfloat16)  54.8 us
    dynamic_update_slice x7, local copies, waits for them, and re-layouts, gather_around(): lax.dynamic_update_slice_in_dim(full, array, (here - far) % ways * step,...  53.3 us
    convert_element_type x1, other arithmetic, local(): x_real = (real_part * line_cos - imag_part * line_sin).astype(jnp.bfloat16)  46.6 us
    reduce_sum x8, other arithmetic, predict(): real_pred = jnp.sum(row_cos * half_cos - row_sin * half_sin, axis=0)  45 us
  transfers between devices with their start and end apart: 8, of which 6 were waited for; matrix products, arithmetic and copies ran while one was open for 16% of the time, Pallas kernels for 0%

profile of v1, /device:TPU:0, one launch (start us, length us, event | category | flops | bytes accessed | tf_op | source)
XLA Modules:
  0.0 1426.6 jit_solution(1274177761151785429)
XLA Ops:
  10.7 8.2 fusion.57
  18.9 34.4 %fusion.32 = (f32[1024,64,32]{0,2,1:T(8,128)}, f32[1024,64,32]{0,2,1:T(8,128)}) fusion(s32[32]{0:T(128)S(1)} %multiply_add_fusion, s32[1024,64]{0,1:T(8,128)S(1)} %broadcast_multiply_fusion), kind=kLoop, calls=%fused_computation.55 | loop fusion | flops 29360128 | bytes 17039488 | tf_op jit(solution)/shard_map/cos | solution.py:43
  53.3 27.3 %add_convert_fusion.1 = (bf16[1024,64,32,8]{0,3,2,1:T(8,128)(2,1)}, bf16[1024,64,32,8]{0,3,2,1:T(8,128)(2,1)}) fusion(f32[1024,64,8]{0,2,1:T(8,128)S(1)} %get-tuple-element.152, f32[1024,64,32]{0,2,1:T(8,128)} %get-tuple-element.148, f32[1024,64,8]{0,2,1:T(8,128)S(1)} %get-tuple-element.151, f32[1024,64,32]{0,2,1:T(8,128)} %get-tuple-element.147), kind=kLoop, calls=%fused_computation.30 | loop fusion | flops 134217728 | bytes 88080384 | tf_op jit(solution)/shard_map/convert_element_type | solution.py:52
  97.6 46.6 %fusion.10 = (bf16[1024,16384]{0,1:T(8,128)(2,1)}, bf16[1024,16384]{0,1:T(8,128)(2,1)}) fusion(bf16[1024,64,32,8]{0,3,2,1:T(8,128)(2,1)} %get-tuple-element.144, bf16[1024,64,32,8]{0,3,2,1:T(8,128)(2,1)} %get-tuple-element.143, f32[1024,256]{0,1:T(8,128)} %copy.24, f32[1024,256]{0,1:T(8,128)S(1)} %copy.23), kind=kLoop, calls=%fused_computation.22 | loop fusion | flops 167772160 | bytes 136314880 | tf_op jit(solution)/shard_map/convert_element_type | solution.py:93
  144.2 28.8 %fusion.22 = bf16[16384,256]{1,0:T(8,128)(2,1)} fusion(bf16[1024,16384]{0,1:T(8,128)(2,1)} %get-tuple-element.140, bf16[1024,16384]{0,1:T(8,128)(2,1)} %get-tuple-element.139, bf16[1024,256]{1,0:T(8,128)(2,1)} %fusion.61, bf16[1024,256]{1,0:T(8,128)(2,1)} %cosine_convert_fusion), kind=kOutput, calls=%fused_computation.36 | convolution fusion | flops 17324572672 | bytes 76546048 | tf_op jit(solution)/shard_map/dot_general | solution.py:97
  173.0 192.4 %all_to_all.36 = bf16[64,256,256]{2,1,0:T(8,128)(2,1)} all-to-all(bf16[64,256,256]{2,1,0:T(8,128)(2,1)} %bitcast.134), channel_id=1, replica_groups=mesh['chan'=4,'tile'=8] {'chan'}, dimensions={0} | all-to-all | bytes 16777216 | tf_op jit(solution)/shard_map/all_to_all | solution.py:108
  365.4 13.7 copy.25
  379.1 14.4 %all_to_all.29 = bf16[16,1024,256]{1,2,0:T(8,128)(2,1)} reshape(bf16[16,4,256,256]{2,1,3,0:T(4,128)(2,1)} %bitcast.131) | data formatting | bytes 16777216 | tf_op jit(solution)/shard_map/all_to_all | solution.py:108
  393.4 14.7 %convert_bitcast_fusion = bf16[16,1024,256]{1,2,0:T(8,128)(2,1)} fusion(bf16[16,1024,256]{1,2,0:T(8,128)(2,1)} %all_to_all.29, bf16[1024,1024]{1,0:T(8,128)(2,1)S(1)} %copy-done), kind=kOutput, calls=%fused_computation.53 | convolution fusion | flops 8594128896 | bytes 18874368 | tf_op jit(solution)/shard_map/fg,qgm->qfm/dot_general | solution.py:105
  408.1 12.6 copy.26
  420.7 190.2 %all_to_all.37 = bf16[16,1024,256]{2,0,1:T(8,128)(2,1)} all-to-all(bf16[16,1024,256]{2,0,1:T(8,128)(2,1)} %copy.26), channel_id=1, replica_groups=mesh['chan'=4,'tile'=8] {'chan'}, dimensions={1} | all-to-all | bytes 16777216 | tf_op jit(solution)/shard_map/all_to_all | solution.py:111
  610.9 9.9 copy.28
  620.8 94.0 %collective-permute-done = bf16[64,256,256]{2,1,0:T(8,128)(2,1)S(1)} collective-permute-done((bf16[64,256,256]{2,1,0:T(8,128)(2,1)}, bf16[64,256,256]{2,1,0:T(8,128)(2,1)S(1)}, u32[]{:S(2)}, u32[]{:S(2)}) %collective-permute-start) | collective-permute-done | bytes 8388640 | tf_op jit(solution)/shard_map/ppermute | solution.py:21
  718.0 93.8 %collective-permute-done.1 = bf16[64,256,256]{2,1,0:T(8,128)(2,1)S(1)} collective-permute-done((bf16[64,256,256]{2,1,0:T(8,128)(2,1)S(1)}, bf16[64,256,256]{2,1,0:T(8,128)(2,1)S(1)}, u32[]{:S(2)}, u32[]{:S(2)}) %collective-permute-start.1) | collective-permute-done | bytes 8388640 | tf_op jit(solution)/shard_map/ppermute | solution.py:21
  815.0 93.8 %collective-permute-done.2 = bf16[64,256,256]{2,1,0:T(8,128)(2,1)S(1)} collective-permute-done((bf16[64,256,256]{2,1,0:T(8,128)(2,1)S(1)}, bf16[64,256,256]{2,1,0:T(8,128)(2,1)S(1)}, u32[]{:S(2)}, u32[]{:S(2)}) %collective-permute-start.2) | collective-permute-done | bytes 8388640 | tf_op jit(solution)/shard_map/ppermute | solution.py:21
  912.0 93.8 %collective-permute-done.3 = bf16[64,256,256]{2,1,0:T(8,128)(2,1)S(1)} collective-permute-done((bf16[64,256,256]{2,1,0:T(8,128)(2,1)S(1)}, bf16[64,256,256]{2,1,0:T(8,128)(2,1)S(1)}, u32[]{:S(2)}, u32[]{:S(2)}) %collective-permute-start.3) | collective-permute-done | bytes 8388640 | tf_op jit(solution)/shard_map/ppermute | solution.py:21
  1009.0 93.9 %collective-permute-done.4 = bf16[64,256,256]{2,1,0:T(8,128)(2,1)} collective-permute-done((bf16[64,256,256]{2,1,0:T(8,128)(2,1)S(1)}, bf16[64,256,256]{2,1,0:T(8,128)(2,1)}, u32[]{:S(2)}, u32[]{:S(2)}) %collective-permute-start.4) | collective-permute-done | bytes 8388640 | tf_op jit(solution)/shard_map/ppermute | solution.py:21
  1104.4 34.7 %fusion.34 = (f32[128,512,32]{0,2,1:T(8,128)}, f32[128,512,32]{0,2,1:T(8,128)}) fusion(s32[32]{0:T(128)S(1)} %copy-done.10, s32[128,512]{0,1:T(8,128)S(1)} %iota_multiply_fusion), kind=kLoop, calls=%fused_computation.57 | loop fusion | flops 29360128 | bytes 17039488 | tf_op jit(solution)/shard_map/cos | solution.py:43
  1139.1 57.9 %collective-permute-done.5 = bf16[64,256,256]{2,1,0:T(8,128)(2,1)} collective-permute-done((bf16[64,256,256]{2,1,0:T(8,128)(2,1)}, bf16[64,256,256]{2,1,0:T(8,128)(2,1)}, u32[]{:S(2)}, u32[]{:S(2)}) %collective-permute-start.5) | collective-permute-done | bytes 8388640 | tf_op jit(solution)/shard_map/ppermute | solution.py:21
  1197.0 8.2 fusion.59
  1205.2 27.5 %fusion.18 = (bf16[128,512,256]{0,2,1:T(8,128)(2,1)}, bf16[128,512,256]{0,2,1:T(8,128)(2,1)}) fusion(f32[128,512,8]{0,2,1:T(8,128)S(1)} %get-tuple-element.154, f32[128,512,32]{0,2,1:T(8,128)} %get-tuple-element.150, f32[128,512,8]{0,2,1:T(8,128)S(1)} %get-tuple-element.153, f32[128,512,32]{0,2,1:T(8,128)} %get-tuple-element.149), kind=kLoop, calls=%fused_computation.34 | loop fusion | flops 134217728 | bytes 88080384 | tf_op jit(solution)/shard_map/convert_element_type | solution.py:52
  1232.7 20.9 %broadcast_in_dim.5 = bf16[512,256,256]{2,1,0:T(8,128)(2,1)} broadcast(bf16[]{:T(256)} %constant.152.clone.1), dimensions={} | broadcast | bytes 67108864 | tf_op jit(solution)/shard_map/broadcast_in_dim | solution.py:18
  1253.6 7.6 constant_dynamic-update-slice_fusion.7
  1261.3 7.6 constant_dynamic-update-slice_fusion.6
  1268.8 7.6 constant_dynamic-update-slice_fusion.5
  1276.5 7.6 constant_dynamic-update-slice_fusion.4
  1284.1 7.6 constant_dynamic-update-slice_fusion.3
  1291.7 7.6 constant_dynamic-update-slice_fusion.2
  1299.3 7.6 constant_dynamic-update-slice_fusion.1
  1306.9 7.6 constant_dynamic-update-slice_fusion
  1314.5 103.0 %while.13 = (s32[]{:T(128)}, f32[128,2,256]{0,2,1:T(8,128)S(1)}, s32[8]{0:T(128)S(1)}, bf16[128,512,256]{0,2,1:T(8,128)(2,1)}, bf16[8,64,256,256]{3,2,1,0:T(8,12...) while((s32[]{:T(128)}, f32[128,2,256]{0,2,1:T(8,128)S(1)}, ...), condition=%wide.region_3.4_spmd.clone, body=%wide.region_0.3_spmd.clone.sunk | while | flops 2168619008 | bytes 51774108 | solution.py:132
  1321.9 5.6 fusion.85
  (91 shorter events, 120.5 us)
Async XLA Ops:
  6.5 386.9 %copy-start = (bf16[1024,1024]{1,0:T(8,128)(2,1)S(1)}, bf16[1024,1024]{1,0:T(8,128)(2,1)}, u32[]{:S(2)}) copy-start(bf16[1024,1024]{1,0:T(8,128)(2,1)} %param.11) | copy-start | bytes 6291460
  6.5 84.3 %all-gather.2.cloned.1.call-start = ((), (), s32[]{:S(2)}) async-start(), calls=%async_computation.2 | async-start | bytes 1179648 | tf_op jit(solution)/shard_map/all_gather | solution.py:87
  9.9 43.4 %copy-start.9 = (s32[32]{0:T(128)}, s32[32]{0:T(128)S(1)}, u32[]{:S(2)}) copy-start(s32[32]{0:T(128)S(1)} %multiply_add_fusion) | copy-start | bytes 388
  53.3 27.3 %copy-start.8 = (s32[1024]{0:T(1024)S(1)}, s32[1024]{0:T(1024)}, u32[]{:S(2)}) copy-start(s32[1024]{0:T(1024)} %param.10) | copy-start | bytes 12292
  610.8 493.5 %copy-start.10 = (s32[32]{0:T(128)S(1)}, s32[32]{0:T(128)}, u32[]{:S(2)}) copy-start(s32[32]{0:T(128)} %copy-done.9) | copy-start | bytes 388
  620.8 94.0 %collective-permute-start = (bf16[64,256,256]{2,1,0:T(8,128)(2,1)}, bf16[64,256,256]{2,1,0:T(8,128)(2,1)S(1)}, u32[]{:S(2)}, u32[]{:S(2)}) collective-permute-start(bf16[64,256,256]{2,1,0:T(8,128)(2,1)} %bitcast.128), channel_id=1, source_target_pairs={{0,1},{1,2},{2,3},{3,4},{4,5},{5,6},{6,7},{7,0},{8,9},{9,10},{10,1... | collective-permute-start | bytes 25165832 | tf_op jit(solution)/shard_map/ppermute | solution.py:21
  714.8 3.2 copy-start.2
  718.0 93.8 %collective-permute-start.1 = (bf16[64,256,256]{2,1,0:T(8,128)(2,1)S(1)}, bf16[64,256,256]{2,1,0:T(8,128)(2,1)S(1)}, u32[]{:S(2)}, u32[]{:S(2)}) collective-permute-start(bf16[64,256,256]{2,1,0:T(8,128)(2,1)S(1)} %collective-permute-done), channel_id=1, source_target_pairs={{0,1},{1,2},{2,3},{3,4},{4,5},{5,6},{6,7},{7,0},{8,9},{9,10},{10,1... | collective-permute-start | bytes 25165832 | tf_op jit(solution)/shard_map/ppermute | solution.py:21
  811.8 3.2 copy-start.3
  815.0 93.8 %collective-permute-start.2 = (bf16[64,256,256]{2,1,0:T(8,128)(2,1)S(1)}, bf16[64,256,256]{2,1,0:T(8,128)(2,1)S(1)}, u32[]{:S(2)}, u32[]{:S(2)}) collective-permute-start(bf16[64,256,256]{2,1,0:T(8,128)(2,1)S(1)} %collective-permute-done.1), channel_id=1, source_target_pairs={{0,1},{1,2},{2,3},{3,4},{4,5},{5,6},{6,7},{7,0},{8,9},{9,10},{10,1... | collective-permute-start | bytes 25165832 | tf_op jit(solution)/shard_map/ppermute | solution.py:21
  908.8 3.2 copy-start.4
  912.0 93.8 %collective-permute-start.3 = (bf16[64,256,256]{2,1,0:T(8,128)(2,1)S(1)}, bf16[64,256,256]{2,1,0:T(8,128)(2,1)S(1)}, u32[]{:S(2)}, u32[]{:S(2)}) collective-permute-start(bf16[64,256,256]{2,1,0:T(8,128)(2,1)S(1)} %collective-permute-done.2), channel_id=1, source_target_pairs={{0,1},{1,2},{2,3},{3,4},{4,5},{5,6},{6,7},{7,0},{8,9},{9,10},{10,1... | collective-permute-start | bytes 25165832 | tf_op jit(solution)/shard_map/ppermute | solution.py:21
  1005.8 3.2 copy-start.5
  1009.0 93.9 %collective-permute-start.4 = (bf16[64,256,256]{2,1,0:T(8,128)(2,1)S(1)}, bf16[64,256,256]{2,1,0:T(8,128)(2,1)}, u32[]{:S(2)}, u32[]{:S(2)}) collective-permute-start(bf16[64,256,256]{2,1,0:T(8,128)(2,1)S(1)} %collective-permute-done.3), channel_id=1, source_target_pairs={{0,1},{1,2},{2,3},{3,4},{4,5},{5,6},{6,7},{7,0},{8,9},{9,10},{10,1... | collective-permute-start | bytes 25165832 | tf_op jit(solution)/shard_map/ppermute | solution.py:21
  1102.9 94.1 %collective-permute-start.5 = (bf16[64,256,256]{2,1,0:T(8,128)(2,1)}, bf16[64,256,256]{2,1,0:T(8,128)(2,1)}, u32[]{:S(2)}, u32[]{:S(2)}) collective-permute-start(bf16[64,256,256]{2,1,0:T(8,128)(2,1)} %collective-permute-done.4), channel_id=1, source_target_pairs={{0,1},{1,2},{2,3},{3,4},{4,5},{5,6},{6,7},{7,0},{8,9},{9,10},{10,1... | collective-permute-start | bytes 25165832 | tf_op jit(solution)/shard_map/ppermute | solution.py:21
  1197.0 110.0 %collective-permute-start.6 = (bf16[64,256,256]{2,1,0:T(8,128)(2,1)}, bf16[64,256,256]{2,1,0:T(8,128)(2,1)}, u32[]{:S(2)}, u32[]{:S(2)}) collective-permute-start(bf16[64,256,256]{2,1,0:T(8,128)(2,1)} %collective-permute-done.5), channel_id=1, source_target_pairs={{0,1},{1,2},{2,3},{3,4},{4,5},{5,6},{6,7},{7,0},{8,9},{9,10},{10,1... | collective-permute-start | bytes 25165832 | tf_op jit(solution)/shard_map/ppermute | solution.py:21
  1314.5 103.2 %copy-start.6 = (bf16[128,2,256]{2,1,0:T(2,128)(2,1)S(1)}, bf16[128,2,256]{2,1,0:T(2,128)(2,1)}, u32[]{:S(2)}) copy-start(bf16[128,2,256]{2,1,0:T(2,128)(2,1)} %param.7) | copy-start | bytes 393220
  1314.5 103.2 %copy-start.7 = (f32[128,256]{1,0:T(8,128)S(1)}, f32[128,256]{1,0:T(8,128)}, u32[]{:S(2)}) copy-start(f32[128,256]{1,0:T(8,128)} %get-tuple-element.137) | copy-start | bytes 393220
  1417.6 1.7 copy-start.1
Sparse Core Ops, SparseCore 0:
  10.0 26.2 all-gather.1
